TPU v7x, 256 devices: a whole 4x4x8 slice. The times are simulated.
256 devices in a mesh: cuts: 64 (over x, y, z_lo), frame: 4 (over z_hi, core).
Axes of the slice: x: 4, y: 4, z: 8 (z_hi: 2, z_lo: 4; z = z_hi * 4 + z_lo), core: 2. Of those that a mesh axis runs over, the one named last changes fastest.
Arguments:
- basis: bfloat16 [2, 32, 128, 4, 256], P(None, None, 'cuts', 'frame'), may hold values from -6 to 6
- coil_maps: bfloat16 [2, 12, 128, 4, 256], P(None, None, 'cuts', 'frame'), may hold values from -3 to 3
- factors: bfloat16 [2, 32, 64], P(None, None, 'frame'), may hold values from -0.75 to 0.75
- lines: int32 [64, 128], P(None, 'cuts'), may hold values from 0 to 511
- kdata: bfloat16 [2, 64, 128, 12, 4], P(None, None, 'cuts', None, 'frame'), may hold values from -6 to 6
Outputs:
- basis_grad: float32 [2, 32, 128, 4, 256], P(None, None, 'cuts', 'frame')
- factor_grad: float32 [2, 32, 64], P(None, None, 'frame')
Inputs may be any that keep to these rules, and one draw needn't show every extreme that they name: lines[t, j] = (ky - (j // 2) * 4) * 128 + kz for a position (ky, kz) sampled in frame t whose ky lies in the rows (j // 2) * 4 to (j // 2 + 1) * 4 - 1; positions may repeat over frames.
All inputs are finite; a program needn't handle non-finite values.
Results may differ from a plain program's by a relative error of at most 0.011.
Values may be sent and summed in bfloat16 or wider, within the bound.
A program may use at most 64 MiB of HBM per device.

v0:
```python
import math
import jax
import jax.numpy as jnp
import numpy as np
from jax import lax
from jax.sharding import PartitionSpec as P

BF = jnp.bfloat16
F32 = jnp.float32


def dft_np(size):
    index = np.arange(size)
    angle = index[:, None] * index[None, :] % size * (2.0 * math.pi / size)
    return (np.cos(angle) / math.sqrt(size), -np.sin(angle) / math.sqrt(size))


def dot(spec, a, b):
    return jnp.einsum(spec, a, b, preferred_element_type=F32)


def body(basis, coil_maps, factors, lines, kdata):
    n_cuts = lax.axis_size("cuts")
    cuts = lax.axis_index("cuts")
    rank, slab, width = (basis.shape[1], basis.shape[2], basis.shape[4])
    coils = coil_maps.shape[1]
    depth = slab * n_cuts
    rows = width // n_cuts
    lpd = lines.shape[1]
    scale = 1.0 / math.sqrt(coils * lpd * n_cuts * basis.shape[3] * lax.axis_size("frame"))
    cy, sy = dft_np(width)
    perm = (np.arange(rows)[:, None] + rows * np.arange(n_cuts)[None, :]).reshape(-1)
    c, s = (cy[:, perm], sy[:, perm])
    table = jnp.asarray(np.block([[c, s], [-s, c]]), BF)
    v = lax.all_gather(factors, "frame", axis=2, tiled=True)
    frames = v.shape[2]
    every = lax.all_gather(lines, "cuts", axis=0)
    kz = every % depth
    row = every // depth
    b = basis[:, :, :, 0].astype(F32)
    m = coil_maps[:, :, :, 0].astype(F32)
    image = jnp.stack(
        [
            m[0][:, :, None] * b[0].transpose(1, 0, 2)[None]
            - m[1][:, :, None] * b[1].transpose(1, 0, 2)[None],
            m[0][:, :, None] * b[1].transpose(1, 0, 2)[None]
            + m[1][:, :, None] * b[0].transpose(1, 0, 2)[None],
        ],
        axis=3,
    ).astype(BF)
    image = image.reshape(coils * slab * rank, 2 * width)
    hybrid = jnp.dot(image, table, preferred_element_type=F32).astype(BF)
    hybrid = hybrid.reshape(coils, slab, rank, 2, width)
    vr, vi = (v[0], v[1])
    mixer = jnp.stack([jnp.stack([vr, -vi]), jnp.stack([vi, vr])])
    mixed = dot("czlpw,qplt->czqtw", hybrid, mixer).reshape(coils, slab, 2, frames, rows, n_cuts)
    zpos = cuts * slab + jnp.arange(slab)
    angle = (kz[None] * zpos[:, None, None, None] % depth).astype(F32) * (2.0 * math.pi / depth)
    pr = (jnp.cos(angle) / math.sqrt(depth)).astype(BF).astype(F32)
    pi = (-jnp.sin(angle) / math.sqrt(depth)).astype(BF).astype(F32)
    pr = pr.transpose(0, 3, 2, 1)
    pi = pi.transpose(0, 3, 2, 1)
    row = row.transpose(2, 1, 0)
    parts = []
    for sample in range(lpd):
        r = row[sample]
        sel = sum((jnp.where(r == k, mixed[:, :, :, :, k], 0.0) for k in range(rows)))
        re = jnp.sum(sel[:, :, 0] * pr[None, :, sample] - sel[:, :, 1] * pi[None, :, sample], 1)
        im = jnp.sum(sel[:, :, 0] * pi[None, :, sample] + sel[:, :, 1] * pr[None, :, sample], 1)
        parts.append(jnp.stack([re, im]))
    part = jnp.stack(parts)
    part = part.transpose(4, 2, 1, 0, 3).reshape(n_cuts, -1).astype(BF)
    pred = lax.psum_scatter(part, "cuts", scatter_dimension=0, tiled=True)
    kd = kdata[..., 0].transpose(3, 0, 2, 1).reshape(1, -1)
    resid = (pred.astype(F32) - kd.astype(F32)).astype(BF)
    whole = lax.all_gather(resid, "cuts", axis=0, tiled=True)
    whole = whole.reshape(n_cuts, coils, 2, lpd, frames).transpose(3, 2, 1, 4, 0).astype(F32)
    spread = 0.0
    for sample in range(lpd):
        x, y = (whole[sample, 0][:, None], whole[sample, 1][:, None])
        re = x * pr[None, :, sample] + y * pi[None, :, sample]
        im = y * pr[None, :, sample] - x * pi[None, :, sample]
        e = jnp.stack([re, im], 2)
        r = row[sample]
        spread = spread + jnp.stack([jnp.where(r == k, e, 0.0) for k in range(rows)], 4)
    spread = spread.astype(BF).reshape(coils, slab, 2, frames, width)
    outer = dot("czlpw,czqtw->plqt", hybrid, spread)
    gv = jnp.stack([outer[0, :, 0] + outer[1, :, 1], outer[0, :, 1] - outer[1, :, 0]])
    unmix = jnp.stack([jnp.stack([vr, vi]), jnp.stack([-vi, vr])])
    zgrad = dot("czptw,qplt->czlqw", spread, unmix).astype(BF)
    zgrad = zgrad.reshape(coils * slab * rank, 2 * width)
    back = lax.dot_general(zgrad, table, (((1,), (1,)), ((), ())), preferred_element_type=F32)
    back = back.reshape(coils, slab, rank, 2, width)
    gr = jnp.sum(m[0][:, :, None] * back[:, :, :, 0] + m[1][:, :, None] * back[:, :, :, 1], 0)
    gi = jnp.sum(m[0][:, :, None] * back[:, :, :, 1] - m[1][:, :, None] * back[:, :, :, 0], 0)
    grad = jnp.stack([gr, gi]).transpose(0, 2, 1, 3)[:, :, :, None]
    shared = lax.psum_scatter(gv * scale, "frame", scatter_dimension=2, tiled=True)
    return (grad, lax.psum(shared, "cuts"))


def solution(mesh):
    placed = (
        P(None, None, "cuts", "frame", None),
        P(None, None, "cuts", "frame", None),
        P(None, None, "frame"),
        P(None, "cuts"),
        P(None, None, "cuts", None, "frame"),
    )
    return jax.shard_map(
        body,
        mesh=mesh,
        in_specs=placed,
        out_specs=(P(None, None, "cuts", "frame", None), P(None, None, "frame")),
        check_vma=False,
    )
```

profile of v0, /device:TPU:0, one launch (start us, length us, event | category | flops | bytes accessed | tf_op | source)
XLA Modules:
  0.0 1550.7 jit_solution(7144732709453119394)
XLA Ops:
  7.2 0.7 copy.101
  7.9 9.1 all_gather.12
  17.1 0.8 convert_element_type.92
  17.9 186.8 %all-gather.1 = s32[64,64,2]{1,2,0:T(2,128)S(1)} all-gather(s32[1,64,2]{1,2,0:T(2,128)} %bitcast.244), channel_id=2, replica_groups=mesh['cuts'=64,'frame'=4] {'cuts'}, dimensions={0}, use_global_device_ids=true | all-gather | bytes 33280 | tf_op jit(solution)/shard_map/all_gather | solution.py:37
  205.0 0.9 convert_element_type.93
  206.7 1.6 subtract_convert_fusion
  208.3 1.8 pad_maximum_fusion.2
  210.9 1.1 reshape.326
  212.6 1.7 convolution_bitcast_fusion
  214.3 4.4 reshape.327
  218.7 12.0 fusion.43
  230.8 0.8 select_add_fusion.1
  232.6 0.8 copy.115
  233.4 1.3 convert_element_type.102
  234.8 0.7 dynamic-slice.2
  236.8 682.6 %all-reduce.4.cloned.1.call-done = bf16[64,3072]{1,0:T(8,128)(2,1)} async-done(((bf16[64,3072]{1,0:T(8,128)(2,1)}), bf16[64,3072]{1,0:T(8,128)(2,1)}) %all-reduce.4.cloned.1.call-update) | async-done | bytes 393232
  919.5 1.4 fusion.40
  920.8 188.8 %all-gather.2 = bf16[64,1,3072]{2,1,0:T(2,128)(2,1)S(1)} all-gather(bf16[1,1,3072]{2,1,0:T(2,128)(2,1)S(1)} %fusion.40), channel_id=1, replica_groups=mesh['cuts'=64,'frame'=4] {'cuts'}, dimensions={0}, use_global_device_ids=true | all-gather | bytes 399360 | tf_op jit(solution)/shard_map/all_gather | solution.py:76
  1109.6 2.2 convert_reduce_fusion
  1111.8 1.1 reshape.329
  1113.0 1.2 fusion.44
  1116.5 3.5 broadcast_select_fusion.3
  1120.1 3.6 broadcast_select_fusion.7
  1123.7 12.3 broadcast_select_fusion.2
  1136.0 14.7 fusion
  1150.7 3.0 reshape.347
  1153.7 3.0 convert_element_type.113
  1156.6 2.6 fusion.11
  1159.7 0.8 copy.124
  1161.1 18.8 %all-reduce.1 = f32[2,32,64]{1,0,2:T(2,128)S(1)} all-reduce(f32[2,32,64]{1,0,2:T(2,128)S(1)} %copy.129), channel_id=4, replica_groups=mesh['cuts'=64,'frame'=4] {'frame'}, use_global_device_ids=true, to_apply=%region_7.8.clone | all-reduce | flops 4096 | bytes 32768
  1180.0 361.6 %psum.7 = f32[2,32,16]{1,0,2:T(2,128)S(1)} all-reduce(f32[2,32,16]{1,0,2:T(2,128)S(1)} %constant_dynamic-slice_fusion), channel_id=1, replica_groups=mesh['cuts'=64,'frame'=4] {'cuts'}, use_global_device_ids=true, to_apply=%region_8.9 | all-reduce | flops 1024 | bytes 8192 | tf_op jit(solution)/shard_map/psum | solution.py:98
  1543.1 0.8 copy.130
  (114 shorter events, 8.7 us)
Async XLA Ops:
  7.2 912.3 %all-reduce.4.cloned.1.call-start = ((), (), s32[]{:S(2)}) async-start(), calls=%async_computation | async-start | bytes 786432
  17.9 190.4 %copy-start.10 = (f32[12,2,256]{2,1,0:T(2,128)}, f32[12,2,256]{2,1,0:T(2,128)S(1)}, u32[]{:S(2)}) copy-start(f32[12,2,256]{2,1,0:T(2,128)S(1)} %get-tuple-element.60) | copy-start | bytes 73732
  17.9 190.4 %copy-start.12 = (f32[12,2,256]{2,1,0:T(2,128)}, f32[12,2,256]{2,1,0:T(2,128)S(1)}, u32[]{:S(2)}) copy-start(f32[12,2,256]{2,1,0:T(2,128)S(1)} %get-tuple-element.61) | copy-start | bytes 73732
  205.0 25.8 %copy-start.14 = (pred[64,64]{1,0:T(8,128)(4,1)}, pred[64,64]{1,0:T(8,128)(4,1)S(1)}, u32[]{:S(2)}) copy-start(pred[64,64]{1,0:T(8,128)(4,1)S(1)} %get-tuple-element.50) | copy-start | bytes 12292
  205.0 25.8 %copy-start.16 = (pred[64,64]{1,0:T(8,128)(4,1)}, pred[64,64]{1,0:T(8,128)(4,1)S(1)}, u32[]{:S(2)}) copy-start(pred[64,64]{1,0:T(8,128)(4,1)S(1)} %get-tuple-element.51) | copy-start | bytes 12292
  205.0 25.8 %copy-start.18 = (pred[64,64]{1,0:T(8,128)(4,1)}, pred[64,64]{1,0:T(8,128)(4,1)S(1)}, u32[]{:S(2)}) copy-start(pred[64,64]{1,0:T(8,128)(4,1)S(1)} %get-tuple-element.52) | copy-start | bytes 12292
  205.0 25.8 %copy-start.20 = (pred[64,64]{1,0:T(8,128)(4,1)}, pred[64,64]{1,0:T(8,128)(4,1)S(1)}, u32[]{:S(2)}) copy-start(pred[64,64]{1,0:T(8,128)(4,1)S(1)} %get-tuple-element.53) | copy-start | bytes 12292
  205.0 25.8 %copy-start.22 = (pred[64,64]{1,0:T(8,128)(4,1)}, pred[64,64]{1,0:T(8,128)(4,1)S(1)}, u32[]{:S(2)}) copy-start(pred[64,64]{1,0:T(8,128)(4,1)S(1)} %get-tuple-element.54) | copy-start | bytes 12292
  205.0 25.8 %copy-start.24 = (pred[64,64]{1,0:T(8,128)(4,1)}, pred[64,64]{1,0:T(8,128)(4,1)S(1)}, u32[]{:S(2)}) copy-start(pred[64,64]{1,0:T(8,128)(4,1)S(1)} %get-tuple-element.55) | copy-start | bytes 12292
  205.0 25.8 %copy-start.26 = (pred[64,64]{1,0:T(8,128)(4,1)}, pred[64,64]{1,0:T(8,128)(4,1)S(1)}, u32[]{:S(2)}) copy-start(pred[64,64]{1,0:T(8,128)(4,1)S(1)} %get-tuple-element.57) | copy-start | bytes 12292
  205.0 25.8 %copy-start.28 = (pred[64,64]{1,0:T(8,128)(4,1)}, pred[64,64]{1,0:T(8,128)(4,1)S(1)}, u32[]{:S(2)}) copy-start(pred[64,64]{1,0:T(8,128)(4,1)S(1)} %get-tuple-element.56) | copy-start | bytes 12292
  206.6 25.0 %copy-start.5 = (f32[2,64,64]{2,1,0:T(8,128)}, f32[2,64,64]{2,1,0:T(8,128)S(1)}, u32[]{:S(2)}) copy-start(f32[2,64,64]{2,1,0:T(8,128)S(1)} %get-tuple-element.42) | copy-start | bytes 98308
  206.6 25.4 %copy-start.1 = (f32[2,64,64]{2,1,0:T(8,128)}, f32[2,64,64]{2,1,0:T(8,128)S(1)}, u32[]{:S(2)}) copy-start(f32[2,64,64]{2,1,0:T(8,128)S(1)} %get-tuple-element.43) | copy-start | bytes 98308
  206.6 25.0 %copy-start.7 = (f32[2,64,64]{2,1,0:T(8,128)}, f32[2,64,64]{2,1,0:T(8,128)S(1)}, u32[]{:S(2)}) copy-start(f32[2,64,64]{2,1,0:T(8,128)S(1)} %get-tuple-element.45) | copy-start | bytes 98308
  206.7 25.4 %copy-start.3 = (f32[2,64,64]{2,1,0:T(8,128)}, f32[2,64,64]{2,1,0:T(8,128)S(1)}, u32[]{:S(2)}) copy-start(f32[2,64,64]{2,1,0:T(8,128)S(1)} %get-tuple-element.44) | copy-start | bytes 98308
  208.3 2.0 copy-start.32
  232.6 2.2 copy-start.34
  232.6 2.8 copy-start.33
  232.6 3.4 copy-start.31
  1114.2 1.3 copy-start.6
  1116.5 3.5 copy-start.27
  1120.0 3.6 copy-start.15
  1120.0 3.6 copy-start.17
  1120.0 3.6 copy-start.19
  1120.1 3.6 copy-start.21
  1120.1 3.6 copy-start.23
  1120.1 3.6 copy-start.25
  1156.6 2.6 copy-start
  1156.6 2.6 copy-start.30
  1159.7 382.5 %copy-start.9 = (bf16[2,256,512,1,1]{2,1,0,4,3:T(8,128)(2,1)S(1)}, bf16[2,256,512,1,1]{2,1,0,4,3:T(8,128)(2,1)}, u32[]{:S(2)}) copy-start(bf16[2,256,512,1,1]{2,1,0,4,3:T(8,128)(2,1)} %constant.75) | copy-start | bytes 1572868
  1161.1 381.7 %copy-start.11 = (f32[12,2,256]{2,1,0:T(2,128)S(1)}, f32[12,2,256]{2,1,0:T(2,128)}, u32[]{:S(2)}) copy-start(f32[12,2,256]{2,1,0:T(2,128)} %copy-done.10) | copy-start | bytes 73732
  1161.1 381.7 %copy-start.13 = (f32[12,2,256]{2,1,0:T(2,128)S(1)}, f32[12,2,256]{2,1,0:T(2,128)}, u32[]{:S(2)}) copy-start(f32[12,2,256]{2,1,0:T(2,128)} %copy-done.12) | copy-start | bytes 73732
  (4 other events, 3.8 us)
Sparse Core Ops, SparseCore 0:
  234.9 684.5 all-reduce.3
where the time goes:
time: 1550 us
  blocking collectives  765 us (49%)
  waiting for transfers between devices  683 us (44%)
  other arithmetic  46.4 us (3%)
  local copies, waits for them, and re-layouts  35 us (2%)
  between operations  15.6 us (1%)
    unnamed x2, waiting for transfers between devices  683 us
    psum x1, blocking collectives, body(): return (grad, lax.psum(shared, 'cuts'))  362 us
    all_gather x1, blocking collectives, body(): whole = lax.all_gather(resid, 'cuts', axis=0, tiled=True)  189 us
    all_gather x1, blocking collectives, body(): every = lax.all_gather(lines, 'cuts', axis=0)  187 us
  transfers between devices with their start and end apart: 1, of which 1 were waited for; matrix products, arithmetic and copies ran while one was open for 0% of the time, Pallas kernels for 0%

commit v1 on v0

--- a/solution.py
+++ b/solution.py
@@ -1,3 +1,4 @@
+import functools
 import math
 import jax
 import jax.numpy as jnp
@@ -7,6 +8,14 @@
 
 BF = jnp.bfloat16
 F32 = jnp.float32
+
+
+def tell_trails(a0, axis_id):
+    h_now = jax.lax.all_gather(a0, axis_name=axis_id).sum(axis=0)
+    return h_now
+
+
+order_zones = functools.partial(tell_trails, axis_id="cuts")
 
 
 def dft_np(size):
@@ -95,7 +104,7 @@
     gi = jnp.sum(m[0][:, :, None] * back[:, :, :, 1] - m[1][:, :, None] * back[:, :, :, 0], 0)
     grad = jnp.stack([gr, gi]).transpose(0, 2, 1, 3)[:, :, :, None]
     shared = lax.psum_scatter(gv * scale, "frame", scatter_dimension=2, tiled=True)
-    return (grad, lax.psum(shared, "cuts"))
+    return (grad, order_zones(shared))
 
 
 def solution(mesh):

time: 1550 us -> 1380 us (0.89)
  blocking collectives: 765 us -> 591 us
    psum x1 -> x0, blocking collectives: 362 us -> none  [body(): return (grad, lax.psum(shared, 'cuts'))]
    all_gather x0 -> x1, blocking collectives: none -> 188 us  [tell_trails(): h_now = jax.lax.all_gather(a0, axis_name=axis_id).sum(axis=0)]
where the time goes in v1:
time: 1380 us
  waiting for transfers between devices  683 us (49%)
  blocking collectives  591 us (43%)
  other arithmetic  47.1 us (3%)
  local copies, waits for them, and re-layouts  34.4 us (2%)
  between operations  15.6 us (1%)
    unnamed x2, waiting for transfers between devices  683 us
    all_gather x1, blocking collectives, body(): whole = lax.all_gather(resid, 'cuts', axis=0, tiled=True)  189 us
    all_gather x1, blocking collectives, tell_trails(): h_now = jax.lax.all_gather(a0, axis_name=axis_id).sum(axis=0)  188 us
    all_gather x1, blocking collectives, body(): every = lax.all_gather(lines, 'cuts', axis=0)  187 us
  transfers between devices with their start and end apart: 1, of which 1 were waited for; matrix products, arithmetic and copies ran while one was open for 0% of the time, Pallas kernels for 0%

profile of v1, /device:TPU:0, one launch (start us, length us, event | category | flops | bytes accessed | tf_op | source)
XLA Modules:
  0.0 1376.7 jit_solution(8971172593265944899)
XLA Ops:
  7.2 0.7 copy.98
  7.9 9.1 all_gather.18
  17.1 0.8 convert_element_type.92
  17.9 186.8 %all-gather.2 = s32[64,64,2]{1,2,0:T(2,128)S(1)} all-gather(s32[1,64,2]{1,2,0:T(2,128)} %bitcast.246), channel_id=2, replica_groups=mesh['cuts'=64,'frame'=4] {'cuts'}, dimensions={0}, use_global_device_ids=true | all-gather | bytes 33280 | tf_op jit(solution)/shard_map/all_gather | solution.py:46
  205.0 0.9 convert_element_type.93
  206.7 1.6 subtract_convert_fusion
  208.3 1.8 pad_maximum_fusion.2
  210.9 1.1 reshape.326
  212.6 1.7 convolution_bitcast_fusion
  214.3 4.4 reshape.327
  218.7 12.0 fusion.43
  230.8 0.8 select_add_fusion.1
  232.6 0.8 copy.112
  233.4 1.3 convert_element_type.102
  236.8 682.6 %all-reduce.4.cloned.1.call-done = bf16[64,3072]{1,0:T(8,128)(2,1)} async-done(((bf16[64,3072]{1,0:T(8,128)(2,1)}), bf16[64,3072]{1,0:T(8,128)(2,1)}) %all-reduce.4.cloned.1.call-update) | async-done | bytes 393232
  919.5 1.4 fusion.40
  920.8 188.8 %all-gather.3 = bf16[64,1,3072]{2,1,0:T(2,128)(2,1)S(1)} all-gather(bf16[1,1,3072]{2,1,0:T(2,128)(2,1)S(1)} %fusion.40), channel_id=1, replica_groups=mesh['cuts'=64,'frame'=4] {'cuts'}, dimensions={0}, use_global_device_ids=true | all-gather | bytes 399360 | tf_op jit(solution)/shard_map/all_gather | solution.py:85
  1109.6 2.2 convert_reduce_fusion
  1111.8 1.1 reshape.329
  1113.0 1.2 fusion.44
  1116.5 3.5 broadcast_select_fusion.3
  1120.1 3.6 broadcast_select_fusion.7
  1123.7 12.3 broadcast_select_fusion.2
  1136.0 14.7 %fusion = bf16[12,2,2,64,4,64]{5,4,3,1,0,2:T(4,128)(2,1)S(1)} fusion(f32[12,2,2,64,1,64]{5,4,3,1,0,2:T(1,128)S(1)} %get-tuple-element.62, f32[12,2,2,64,1,64]{5,4,3,1,0,2:T(1,128)S(1)} %get-tuple-element.63, f32[12,2,2,64,1,64]{5,4,3,1,0,2:T(1,128)S(1)} %get-tuple-element.64, f32[12,2,2,64,1,64]{5,4,3,1,0,2:T(1,128)S(1)} %get-tuple-element.12, ...), kind=kLoop, calls=%fused_computation.1 | loop fusion | flops 6291456 | bytes 7864320 | tf_op jit(solution)/shard_map/convert_element_type | solution.py:95
  1150.7 3.0 reshape.348
  1153.7 3.0 convert_element_type.113
  1156.6 2.6 fusion.11
  1159.7 0.8 copy.121
  1161.1 18.7 %all-reduce.1 = f32[2,32,64]{1,0,2:T(2,128)S(1)} all-reduce(f32[2,32,64]{1,0,2:T(2,128)S(1)} %copy.126), channel_id=5, replica_groups=mesh['cuts'=64,'frame'=4] {'frame'}, use_global_device_ids=true, to_apply=%region_7.8.clone | all-reduce | flops 4096 | bytes 32768
  1180.7 0.8 copy.129
  1181.5 187.7 %all-gather.1 = f32[128,32,16]{1,2,0:T(8,128)S(1)} all-gather(f32[2,32,16]{1,2,0:T(8,128)S(1)} %copy.127), channel_id=3, replica_groups=mesh['cuts'=64,'frame'=4] {'cuts'}, dimensions={0}, use_global_device_ids=true | all-gather | bytes 266240 | tf_op jit(solution)/shard_map/all_gather | solution.py:14
  1369.2 0.7 reduce_sum.69
  (115 shorter events, 8.8 us)
Async XLA Ops:
  7.2 912.3 %all-reduce.4.cloned.1.call-start = ((), (), s32[]{:S(2)}) async-start(), calls=%async_computation | async-start | bytes 786432
  17.9 190.4 %copy-start.10 = (f32[12,2,256]{2,1,0:T(2,128)}, f32[12,2,256]{2,1,0:T(2,128)S(1)}, u32[]{:S(2)}) copy-start(f32[12,2,256]{2,1,0:T(2,128)S(1)} %get-tuple-element.54) | copy-start | bytes 73732
  17.9 190.4 %copy-start.12 = (f32[12,2,256]{2,1,0:T(2,128)}, f32[12,2,256]{2,1,0:T(2,128)S(1)}, u32[]{:S(2)}) copy-start(f32[12,2,256]{2,1,0:T(2,128)S(1)} %get-tuple-element.55) | copy-start | bytes 73732
  205.0 25.8 %copy-start.14 = (pred[64,64]{1,0:T(8,128)(4,1)}, pred[64,64]{1,0:T(8,128)(4,1)S(1)}, u32[]{:S(2)}) copy-start(pred[64,64]{1,0:T(8,128)(4,1)S(1)} %get-tuple-element.44) | copy-start | bytes 12292
  205.0 25.8 %copy-start.16 = (pred[64,64]{1,0:T(8,128)(4,1)}, pred[64,64]{1,0:T(8,128)(4,1)S(1)}, u32[]{:S(2)}) copy-start(pred[64,64]{1,0:T(8,128)(4,1)S(1)} %get-tuple-element.45) | copy-start | bytes 12292
  205.0 25.8 %copy-start.18 = (pred[64,64]{1,0:T(8,128)(4,1)}, pred[64,64]{1,0:T(8,128)(4,1)S(1)}, u32[]{:S(2)}) copy-start(pred[64,64]{1,0:T(8,128)(4,1)S(1)} %get-tuple-element.46) | copy-start | bytes 12292
  205.0 25.8 %copy-start.20 = (pred[64,64]{1,0:T(8,128)(4,1)}, pred[64,64]{1,0:T(8,128)(4,1)S(1)}, u32[]{:S(2)}) copy-start(pred[64,64]{1,0:T(8,128)(4,1)S(1)} %get-tuple-element.47) | copy-start | bytes 12292
  205.0 25.8 %copy-start.22 = (pred[64,64]{1,0:T(8,128)(4,1)}, pred[64,64]{1,0:T(8,128)(4,1)S(1)}, u32[]{:S(2)}) copy-start(pred[64,64]{1,0:T(8,128)(4,1)S(1)} %get-tuple-element.48) | copy-start | bytes 12292
  205.0 25.8 %copy-start.24 = (pred[64,64]{1,0:T(8,128)(4,1)}, pred[64,64]{1,0:T(8,128)(4,1)S(1)}, u32[]{:S(2)}) copy-start(pred[64,64]{1,0:T(8,128)(4,1)S(1)} %get-tuple-element.49) | copy-start | bytes 12292
  205.0 25.8 %copy-start.26 = (pred[64,64]{1,0:T(8,128)(4,1)}, pred[64,64]{1,0:T(8,128)(4,1)S(1)}, u32[]{:S(2)}) copy-start(pred[64,64]{1,0:T(8,128)(4,1)S(1)} %get-tuple-element.51) | copy-start | bytes 12292
  205.0 25.8 %copy-start.28 = (pred[64,64]{1,0:T(8,128)(4,1)}, pred[64,64]{1,0:T(8,128)(4,1)S(1)}, u32[]{:S(2)}) copy-start(pred[64,64]{1,0:T(8,128)(4,1)S(1)} %get-tuple-element.50) | copy-start | bytes 12292
  206.6 25.0 %copy-start.5 = (f32[2,64,64]{2,1,0:T(8,128)}, f32[2,64,64]{2,1,0:T(8,128)S(1)}, u32[]{:S(2)}) copy-start(f32[2,64,64]{2,1,0:T(8,128)S(1)} %get-tuple-element.36) | copy-start | bytes 98308
  206.6 25.4 %copy-start.1 = (f32[2,64,64]{2,1,0:T(8,128)}, f32[2,64,64]{2,1,0:T(8,128)S(1)}, u32[]{:S(2)}) copy-start(f32[2,64,64]{2,1,0:T(8,128)S(1)} %get-tuple-element.37) | copy-start | bytes 98308
  206.6 25.0 %copy-start.7 = (f32[2,64,64]{2,1,0:T(8,128)}, f32[2,64,64]{2,1,0:T(8,128)S(1)}, u32[]{:S(2)}) copy-start(f32[2,64,64]{2,1,0:T(8,128)S(1)} %get-tuple-element.39) | copy-start | bytes 98308
  206.7 25.4 %copy-start.3 = (f32[2,64,64]{2,1,0:T(8,128)}, f32[2,64,64]{2,1,0:T(8,128)S(1)}, u32[]{:S(2)}) copy-start(f32[2,64,64]{2,1,0:T(8,128)S(1)} %get-tuple-element.38) | copy-start | bytes 98308
  208.3 2.0 copy-start.32
  232.6 2.2 copy-start.34
  232.6 2.8 copy-start.33
  232.6 3.4 copy-start.31
  1114.2 1.3 copy-start.6
  1116.5 3.5 copy-start.27
  1120.0 3.6 copy-start.15
  1120.0 3.6 copy-start.17
  1120.0 3.6 copy-start.19
  1120.1 3.6 copy-start.21
  1120.1 3.6 copy-start.23
  1120.1 3.6 copy-start.25
  1156.6 2.6 copy-start
  1156.6 2.6 copy-start.30
  1159.7 20.2 %copy-start.9 = (bf16[2,256,512,1,1]{2,1,0,4,3:T(8,128)(2,1)S(1)}, bf16[2,256,512,1,1]{2,1,0,4,3:T(8,128)(2,1)}, u32[]{:S(2)}) copy-start(bf16[2,256,512,1,1]{2,1,0,4,3:T(8,128)(2,1)} %constant.75) | copy-start | bytes 1572868
  1161.0 19.4 %copy-start.11 = (f32[12,2,256]{2,1,0:T(2,128)S(1)}, f32[12,2,256]{2,1,0:T(2,128)}, u32[]{:S(2)}) copy-start(f32[12,2,256]{2,1,0:T(2,128)} %copy-done.10) | copy-start | bytes 73732
  1161.0 19.4 %copy-start.13 = (f32[12,2,256]{2,1,0:T(2,128)S(1)}, f32[12,2,256]{2,1,0:T(2,128)}, u32[]{:S(2)}) copy-start(f32[12,2,256]{2,1,0:T(2,128)} %copy-done.12) | copy-start | bytes 73732
  (4 other events, 3.8 us)
Sparse Core Ops, SparseCore 0:
  234.9 684.5 all-reduce.3
